TPU v7x, 32 devices: a whole 2x2x4 slice. The times are simulated.
32 devices in a mesh: groups: 2 (over y), expert: 8 (over z, x), tensor: 2 (over core).
Axes of the slice: x: 2, y: 2, z: 4, core: 2. Of those that a mesh axis runs over, the one named last changes fastest.
Arguments:
- conv_input: bfloat16 [32, 8192], P(('groups', 'expert'), 'tensor'), parts along dimension 0, may hold values from -6 to 6
- gate_input: bfloat16 [32, 8192], P(('groups', 'expert'), 'tensor'), parts along dimension 0, may hold values from -6 to 6
- step_input: bfloat16 [32, 8192], P(('groups', 'expert'), 'tensor'), parts along dimension 0, may hold values from -6 to 6
- b_proj: float32 [32, 16], P(('groups', 'expert')), parts along dimension 0, may hold values from -6 to 6
- c_proj: float32 [32, 16], P(('groups', 'expert')), parts along dimension 0, may hold values from -6 to 6
- slot_ids: int32 [32], P(('groups', 'expert')), parts along dimension 0, may hold values from 0 to 15, as said below
- state_pool: bfloat16 [32, 16, 8192], P(('groups', 'expert'), None, 'tensor'), parts along dimension 0, may hold values from -6 to 6
- conv_pool: bfloat16 [32, 3, 8192], P(('groups', 'expert'), None, 'tensor'), parts along dimension 0, may hold values from -6 to 6
- conv_weight: float32 [4, 8192], P(None, 'tensor'), may hold values from -4 to 4
- conv_bias: float32 [8192], P('tensor'), may hold values from -4 to 4
- step_bias: float32 [8192], P('tensor'), may hold values from -4 to 0
- a_log: float32 [16, 8192], P(None, 'tensor'), may hold values from -1 to 2.5
- d_skip: float32 [8192], P('tensor'), may hold values from 0.5 to 1.5
- out_weight: bfloat16 [8192, 4096], P('tensor', 'expert'), may hold values from -0.0625 to 0.0625
- residual: bfloat16 [32, 4096], P(('groups', 'expert')), parts along dimension 0, may hold values from -6 to 6
- norm_gain: float32 [4096], replicated, may hold values from 0.5 to 1.5
- expert_ids: int32 [32, 2], P(('groups', 'expert')), parts along dimension 0, may hold values from 0 to 2, all different within a row
- expert_probs: bfloat16 [32, 2], P(('groups', 'expert')), parts along dimension 0, may hold values from 0.19921875 to 1
- gate_weight: bfloat16 [36864, 4096], P(('expert', 'tensor')), may hold values from -0.09375 to 0.09375
- up_weight: bfloat16 [36864, 4096], P(('expert', 'tensor')), may hold values from -0.09375 to 0.09375
- down_weight: bfloat16 [36864, 4096], P(('expert', 'tensor')), may hold values from -0.0546875 to 0.0546875
Outputs:
- layer_out: bfloat16 [32, 4096], P(('groups', 'expert')), parts along dimension 0
- new_state: bfloat16 [32, 16, 8192], P(('groups', 'expert'), None, 'tensor'), parts along dimension 0
There are 2 independent parts, one for each index of `groups`. A program takes and returns all parts, laid end to end along the dimension named above; an argument that names none is the same for every part. Nothing has to cross between parts.
Inputs may be any that keep to these rules, and one draw needn't show every extreme that they name: `slot_ids`: the rows of one index of expert (rows d*2 to (d+1)*2 - 1) use distinct slots among d*2 to (d+1)*2 - 1. `expert_ids`: each row names two different experts.
All inputs are finite; a program needn't handle non-finite values.
Results may differ from a plain program's by a relative error of at most 0.0063.
Values may be sent and summed in bfloat16 or wider, within the bound.
A program may use at most 128 MiB of HBM per device.

v0:
```python
import jax
import jax.numpy as jnp
from jax import lax
from jax.sharding import PartitionSpec as P

EXPERTS = 3
FF = 12288


def mamba_step(
    states,
    history,
    conv_input,
    gate_input,
    step_input,
    b_proj,
    c_proj,
    conv_weight,
    conv_bias,
    step_bias,
    a_log,
    d_skip,
):
    inputs = conv_input.astype(jnp.float32)
    conv_sum = conv_weight[-1] * inputs + conv_bias
    for lag in range(history.shape[1]):
        conv_sum = conv_sum + conv_weight[lag] * history[:, lag]
    conv_out = jax.nn.silu(conv_sum)
    step_size = jax.nn.softplus(step_input.astype(jnp.float32) + step_bias)
    state_rates = -jnp.exp(a_log)
    decay_rate = jnp.exp(step_size[:, None, :] * state_rates[None])
    state_next = decay_rate * states + (step_size * conv_out)[:, None, :] * b_proj[:, :, None]
    output = jnp.sum(c_proj[:, :, None] * state_next, axis=1) + d_skip * conv_out
    gated_out = (output * jax.nn.silu(gate_input.astype(jnp.float32))).astype(jnp.bfloat16)
    return (state_next, gated_out)


def expert_terms(rows, coefs, first_unit, gate_weight, up_weight, down_weight):
    dims = (((1,), (1,)), ((), ()))
    gate_act = lax.dot_general(rows, gate_weight, dims, preferred_element_type=jnp.float32)
    up_act = lax.dot_general(rows, up_weight, dims, preferred_element_type=jnp.float32)
    hidden = (jax.nn.silu(gate_act) * up_act).astype(jnp.bfloat16)
    units = gate_weight.shape[0]
    lower_expert = first_unit // FF
    boundary = (lower_expert + 1) * FF - first_unit
    column = jnp.arange(units, dtype=jnp.int32)[None, :]
    zeros_bf = jnp.zeros_like(hidden)
    lower_hidden = jnp.where(column < boundary, hidden, zeros_bf)
    upper_hidden = jnp.where(column >= boundary, hidden, zeros_bf)
    expert_range = jnp.arange(EXPERTS, dtype=jnp.int32)[None, :]
    wide_coefs = coefs.astype(jnp.float32)
    lower_coef = jnp.sum(wide_coefs * (expert_range == lower_expert).astype(jnp.float32), axis=1)
    upper_coef = jnp.sum(
        wide_coefs * (expert_range == lower_expert + 1).astype(jnp.float32), axis=1
    )
    lower_out = jnp.dot(lower_hidden, down_weight, preferred_element_type=jnp.float32)
    upper_out = jnp.dot(upper_hidden, down_weight, preferred_element_type=jnp.float32)
    return lower_coef[:, None] * lower_out + upper_coef[:, None] * upper_out


def local(
    conv_input,
    gate_input,
    step_input,
    b_proj,
    c_proj,
    slot_ids,
    state_pool,
    conv_pool,
    conv_weight,
    conv_bias,
    step_bias,
    a_log,
    d_skip,
    out_weight,
    residual,
    norm_gain,
    expert_ids,
    expert_probs,
    gate_weight,
    up_weight,
    down_weight,
):
    pool_dev = state_pool.shape[0]
    local_slot = slot_ids - lax.axis_index("expert") * pool_dev
    select = (local_slot[:, None] == jnp.arange(pool_dev, dtype=jnp.int32)[None, :]).astype(
        jnp.bfloat16
    )
    states = jnp.einsum("rp,pnc->rnc", select, state_pool, preferred_element_type=jnp.float32)
    history = jnp.einsum("rp,pkc->rkc", select, conv_pool, preferred_element_type=jnp.float32)
    state_next, gated_out = mamba_step(
        states,
        history,
        conv_input,
        gate_input,
        step_input,
        b_proj,
        c_proj,
        conv_weight,
        conv_bias,
        step_bias,
        a_log,
        d_skip,
    )
    columns = jnp.dot(
        lax.all_gather(gated_out, "expert", axis=0, tiled=True),
        out_weight,
        preferred_element_type=jnp.float32,
    )
    returned_cols = lax.all_to_all(columns, "expert", split_axis=0, concat_axis=1, tiled=True)
    mixed = lax.psum(returned_cols, "tensor").astype(jnp.bfloat16)
    hidden_state = (residual.astype(jnp.float32) + mixed.astype(jnp.float32)).astype(jnp.bfloat16)
    wide = hidden_state.astype(jnp.float32)
    normed = (
        wide * lax.rsqrt(jnp.mean(wide * wide, axis=1, keepdims=True) + 1e-05) * norm_gain
    ).astype(jnp.bfloat16)
    probs = expert_probs.astype(jnp.float32)
    expert_range = jnp.arange(EXPERTS, dtype=jnp.int32)
    picked = (expert_ids[:, :, None] == expert_range[None, None, :]).astype(jnp.float32)
    coefs = jnp.sum(picked * probs[:, :, None], axis=1).astype(jnp.bfloat16)
    units = gate_weight.shape[0]
    first_unit = (
        lax.axis_index("expert") * lax.axis_size("tensor") + lax.axis_index("tensor")
    ) * units
    peers = lax.axis_size("expert")
    span = EXPERTS * FF // peers
    dest = jnp.arange(peers, dtype=jnp.int32)[:, None]
    intersection = (
        (expert_range[None, :] * FF < (dest + 1) * span)
        & ((expert_range[None, :] + 1) * FF > dest * span)
    ).astype(jnp.float32)
    chosen = jnp.sum(picked, axis=1)
    needed = jnp.dot(intersection, chosen.T, preferred_element_type=jnp.float32) > 0.5
    outgoing = jnp.where(needed[:, :, None], normed[None], jnp.zeros_like(normed)[None])
    out_coefs = jnp.broadcast_to(coefs[None], (peers, coefs.shape[0], coefs.shape[1]))
    rows_in = lax.all_to_all(outgoing, "expert", split_axis=0, concat_axis=0, tiled=True)
    coefs_in = lax.all_to_all(out_coefs, "expert", split_axis=0, concat_axis=0, tiled=True)
    flat_rows = rows_in.reshape(-1, rows_in.shape[2])
    flat_coefs = coefs_in.reshape(-1, coefs_in.shape[2])
    result = expert_terms(flat_rows, flat_coefs, first_unit, gate_weight, up_weight, down_weight)
    partial_value = result.reshape(rows_in.shape[0], rows_in.shape[1], rows_in.shape[2])
    returned = lax.all_to_all(partial_value, "expert", split_axis=0, concat_axis=0, tiled=True)
    routed = lax.psum(jnp.sum(returned, axis=0), "tensor")
    layer_out = (hidden_state.astype(jnp.float32) + routed).astype(jnp.bfloat16)
    return (layer_out, state_next.astype(jnp.bfloat16))


def solution(mesh):
    return jax.shard_map(
        local,
        mesh=mesh,
        in_specs=(
            P(("groups", "expert"), "tensor"),
            P(("groups", "expert"), "tensor"),
            P(("groups", "expert"), "tensor"),
            P(("groups", "expert"), None),
            P(("groups", "expert"), None),
            P(("groups", "expert")),
            P(("groups", "expert"), None, "tensor"),
            P(("groups", "expert"), None, "tensor"),
            P(None, "tensor"),
            P("tensor"),
            P("tensor"),
            P(None, "tensor"),
            P("tensor"),
            P("tensor", "expert"),
            P(("groups", "expert"), None),
            P(),
            P(("groups", "expert"), None),
            P(("groups", "expert"), None),
            P(("expert", "tensor"), None),
            P(("expert", "tensor"), None),
            P(("expert", "tensor"), None),
        ),
        out_specs=(P(("groups", "expert"), None), P(("groups", "expert"), None, "tensor")),
        check_vma=False,
    )
```

profile of v0, /device:TPU:0, one launch (start us, length us, event | category | flops | bytes accessed | tf_op | source)
XLA Modules:
  0.0 134.9 jit_solution(396333789273066836)
XLA Ops:
  0.6 0.0 copy-start
  0.7 0.8 copy.73
  1.4 0.8 copy.71
  2.2 1.1 fusion.39
  3.3 1.0 exponential_negate_fusion
  4.3 0.7 broadcast_subtract_fusion
  4.9 1.0 fusion.32
  6.0 0.9 fusion.37
  6.9 0.0 copy-done
  6.9 1.1 fusion.38
  8.0 0.8 fusion.24
  8.8 32.3 %all-gather = bf16[8,2,4096]{2,1,0:T(2,128)(2,1)S(1)} all-gather(bf16[1,2,4096]{2,1,0:T(2,128)(2,1)S(1)} %fusion.24), channel_id=1, replica_groups=mesh['groups'=2,'expert'=8,'tensor'=2] {'expert'}, dimensions={0}, use_global_device_ids=true | all-gather | bytes 147456 | tf_op jit(solution)/shard_map/all_gather | solution.py:106
  41.2 0.1 reshape.106
  41.2 2.8 %fusion.40 = f32[16,512]{1,0:T(8,128)S(1)} fusion(bf16[16,4096]{1,0:T(8,128)(2,1)S(1)} %reshape.106, bf16[4096,512]{1,0:T(8,128)(2,1)} %param.34), kind=kOutput, calls=%fused_computation.76 | convolution fusion | flops 67108864 | bytes 4358144 | tf_op jit(solution)/shard_map/dot_general | solution.py:105
  44.0 0.7 all_to_all.23
  44.7 5.5 %all-to-all-start = ((f32[8,2,512]{2,1,0:T(2,128)}), f32[8,2,512]{2,1,0:T(2,128)S(1)}, u32[]{:S(2)}, u32[]{:S(2)}) async-start(f32[8,2,512]{2,1,0:T(2,128)} %all_to_all.23), calls=%async_computation | async-start | bytes 65536 | tf_op jit(solution)/shard_map/all_to_all | solution.py:110
  50.2 0.7 convert_element_type.85
  50.8 0.8 convert_reduce_fusion
  51.6 0.2 convolution_compare_fusion
  51.8 0.1 copy.77
  51.9 5.0 %all-to-all-done = f32[8,2,512]{2,1,0:T(2,128)S(1)} async-done(((f32[8,2,512]{2,1,0:T(2,128)}), f32[8,2,512]{2,1,0:T(2,128)S(1)}, u32[]{:S(2)}, u32[]{:S(2)}) %all-to-all-start) | async-done | bytes 32800 | tf_op jit(solution)/shard_map/all_to_all | solution.py:110
  56.8 0.6 broadcast_in_dim.29
  57.4 3.3 %all-to-all-start.1 = ((bf16[8,2,3]{2,1,0:T(2,128)(2,1)}), bf16[8,2,3]{2,1,0:T(2,128)(2,1)S(1)}, u32[]{:S(2)}, u32[]{:S(2)}) async-start(bf16[8,2,3]{2,1,0:T(2,128)(2,1)} %broadcast_in_dim.29), calls=%async_computation.1 | async-start | bytes 8192 | tf_op jit(solution)/shard_map/all_to_all | solution.py:137
  60.8 3.4 %psum.14 = bf16[2,4096]{1,0:T(2,128)(2,1)S(1)} all-reduce(f32[2,4096]{1,0:T(2,128)S(1)} %bitcast.56), channel_id=1, replica_groups=mesh['groups'=2,'expert'=8,'tensor'=2] {'tensor'}, use_global_device_ids=true, to_apply=%region_1.2 | all-reduce | flops 8192 | bytes 49152 | tf_op jit(solution)/shard_map/psum | solution.py:111
  64.2 0.9 fusion.13
  65.0 0.8 fusion.15
  65.9 0.8 broadcast_select_fusion
  66.7 0.4 all-to-all-done.1
  67.1 5.5 %all-to-all-start.2 = ((bf16[8,2,4096]{2,1,0:T(2,128)(2,1)}), bf16[8,2,4096]{2,1,0:T(2,128)(2,1)S(1)}, u32[]{:S(2)}, u32[]{:S(2)}) async-start(bf16[8,2,4096]{2,1,0:T(2,128)(2,1)} %broadcast_select_fusion), calls=%async_computation.2 | async-start | bytes 262144 | tf_op jit(solution)/shard_map/all_to_all | solution.py:136
  72.6 0.1 copy.75
  72.7 0.1 fusion.27
  72.8 0.1 copy.78
  72.9 0.1 mul.262
  73.0 0.1 copy.76
  73.1 0.1 mul.245
  73.1 6.9 %all-to-all-done.2 = bf16[8,2,4096]{2,1,0:T(2,128)(2,1)S(1)} async-done(((bf16[8,2,4096]{2,1,0:T(2,128)(2,1)}), bf16[8,2,4096]{2,1,0:T(2,128)(2,1)S(1)}, u32[]{:S(2)}, u32[]{:S(2)}) %all-to-all-start.2) | async-done | bytes 131104 | tf_op jit(solution)/shard_map/all_to_all | solution.py:136
  80.1 0.1 reshape.103
  80.1 11.3 %fusion.41 = f32[16,2304]{1,0:T(8,128)S(1)} fusion(bf16[16,4096]{1,0:T(8,128)(2,1)S(1)} %reshape.103, bf16[2304,4096]{1,0:T(8,128)(2,1)} %param.39), kind=kOutput, calls=%fused_computation.77 | convolution fusion | flops 301989888 | bytes 19152896 | tf_op jit(solution)/shard_map/dot_general | solution.py:40
  91.5 11.3 %fusion.2 = bf16[16,2304]{1,0:T(8,128)(2,1)S(1)} fusion(bf16[16,4096]{1,0:T(8,128)(2,1)S(1)} %reshape.103, bf16[2304,4096]{1,0:T(8,128)(2,1)} %param.40, f32[16,2304]{1,0:T(8,128)S(1)} %fusion.41), kind=kOutput, calls=%fused_computation.6 | convolution fusion | flops 302211072 | bytes 19226624 | tf_op jit(solution)/shard_map/dot_general | solution.py:41
  102.8 7.7 %convolution_multiply_fusion.2 = f32[16,4096]{1,0:T(8,128)S(1)} fusion(bf16[2304,4096]{1,0:T(8,128)(2,1)} %param.41, f32[16]{0:T(128)S(1)} %mul.245, bf16[16,2304]{1,0:T(8,128)(2,1)S(1)} %fusion.2, pred[2304]{0:T(1024)(128)(4,1)S(1)} %get-tuple-element.38), kind=kOutput, calls=%fused_computation.4 | convolution fusion | flops 302092288 | bytes 19212608 | tf_op jit(solution)/shard_map/dot_general | solution.py:56
  110.5 7.7 %fusion.1 = f32[16,4096]{1,0:T(8,128)S(1)} fusion(f32[16,4096]{1,0:T(8,128)S(1)} %convolution_multiply_fusion.2, bf16[2304,4096]{1,0:T(8,128)(2,1)} %param.41, f32[16]{0:T(128)S(1)} %mul.262, bf16[16,2304]{1,0:T(8,128)(2,1)S(1)} %fusion.2, pred[2304]{0:T(1024)(128)(4,1)S(1)} %get-tuple-element.37), kind=kOutput, calls=%fused_computation.3 | convolution fusion | flops 302157824 | bytes 19474752 | tf_op jit(solution)/shard_map/dot_general | solution.py:57
  118.2 0.8 reshape.104
  119.1 3.4 %all-to-all-start.3 = ((f32[8,2,4096]{2,1,0:T(2,128)}), f32[8,2,4096]{2,1,0:T(2,128)S(1)}, u32[]{:S(2)}, u32[]{:S(2)}) async-start(f32[8,2,4096]{2,1,0:T(2,128)} %reshape.104), calls=%async_computation.3 | async-start | bytes 524288 | tf_op jit(solution)/shard_map/all_to_all | solution.py:142
  122.5 0.9 copy.79
  123.4 7.4 %all-to-all-done.3 = f32[8,2,4096]{2,1,0:T(2,128)S(1)} async-done(((f32[8,2,4096]{2,1,0:T(2,128)}), f32[8,2,4096]{2,1,0:T(2,128)S(1)}, u32[]{:S(2)}, u32[]{:S(2)}) %all-to-all-start.3) | async-done | bytes 262176 | tf_op jit(solution)/shard_map/all_to_all | solution.py:142
  130.8 0.1 reduce_sum.69
  130.9 3.4 %psum.15 = f32[2,4096]{1,0:T(2,128)S(1)} all-reduce(f32[2,4096]{1,0:T(2,128)S(1)} %reduce_sum.69), channel_id=1, replica_groups=mesh['groups'=2,'expert'=8,'tensor'=2] {'tensor'}, use_global_device_ids=true, to_apply=%region_8.9 | all-reduce | flops 8192 | bytes 65536 | tf_op jit(solution)/shard_map/psum | solution.py:143
  134.3 0.6 fusion.16
  (5 shorter events, 0.0 us)
Async XLA Ops:
  0.6 6.3 %copy-start = (bf16[2,16,4096]{2,1,0:T(8,128)(2,1)S(1)}, bf16[2,16,4096]{2,1,0:T(8,128)(2,1)}, u32[]{:S(2)}) copy-start(bf16[2,16,4096]{2,1,0:T(8,128)(2,1)} %param.27) | copy-start | bytes 786436
  44.7 12.1 %all-to-all-start = ((f32[8,2,512]{2,1,0:T(2,128)}), f32[8,2,512]{2,1,0:T(2,128)S(1)}, u32[]{:S(2)}, u32[]{:S(2)}) async-start(f32[8,2,512]{2,1,0:T(2,128)} %all_to_all.23), calls=%async_computation | async-start | bytes 65536 | tf_op jit(solution)/shard_map/all_to_all | solution.py:110
  57.4 9.7 %all-to-all-start.1 = ((bf16[8,2,3]{2,1,0:T(2,128)(2,1)}), bf16[8,2,3]{2,1,0:T(2,128)(2,1)S(1)}, u32[]{:S(2)}, u32[]{:S(2)}) async-start(bf16[8,2,3]{2,1,0:T(2,128)(2,1)} %broadcast_in_dim.29), calls=%async_computation.1 | async-start | bytes 8192 | tf_op jit(solution)/shard_map/all_to_all | solution.py:137
  67.1 13.0 %all-to-all-start.2 = ((bf16[8,2,4096]{2,1,0:T(2,128)(2,1)}), bf16[8,2,4096]{2,1,0:T(2,128)(2,1)S(1)}, u32[]{:S(2)}, u32[]{:S(2)}) async-start(bf16[8,2,4096]{2,1,0:T(2,128)(2,1)} %broadcast_select_fusion), calls=%async_computation.2 | async-start | bytes 262144 | tf_op jit(solution)/shard_map/all_to_all | solution.py:136
  119.1 11.7 %all-to-all-start.3 = ((f32[8,2,4096]{2,1,0:T(2,128)}), f32[8,2,4096]{2,1,0:T(2,128)S(1)}, u32[]{:S(2)}, u32[]{:S(2)}) async-start(f32[8,2,4096]{2,1,0:T(2,128)} %reshape.104), calls=%async_computation.3 | async-start | bytes 524288 | tf_op jit(solution)/shard_map/all_to_all | solution.py:142
where the time goes:
time: 136 us; the launch traced here: 135 us
  matrix products  43.3 us (32%)
  blocking collectives  39.2 us (29%)
  waiting for transfers between devices  19.8 us (15%)
  starting transfers between devices  17.7 us (13%)
  other arithmetic  8.12 us (6%)
  local copies, waits for them, and re-layouts  6.19 us (5%)
    all_gather x1, blocking collectives, local(): lax.all_gather(gated_out, 'expert', axis=0, tiled=True)  32.3 us
    dot_general x1, matrix products, expert_terms(): lax.dot_general(rows, up_weight, dims, preferred_element_type=jnp.float32)  11.3 us
    dot_general x1, matrix products, expert_terms(): lax.dot_general(rows, gate_weight, dims, preferred_element_type=jnp.float32)  11.3 us
    dot_general x1, matrix products, expert_terms(): jnp.dot(lower_hidden, down_weight, preferred_element_type=jnp.float32)  7.7 us
    dot_general x1, matrix products, expert_terms(): jnp.dot(upper_hidden, down_weight, preferred_element_type=jnp.float32)  7.7 us
    all_to_all x1, waiting for transfers between devices, local(): lax.all_to_all(partial_value, 'expert', split_axis=0, concat_axis=0, tile...  7.44 us
    all_to_all x1, waiting for transfers between devices, local(): lax.all_to_all(outgoing, 'expert', split_axis=0, concat_axis=0, tiled=True)  6.94 us
    all_to_all x1, starting transfers between devices, local(): lax.all_to_all(outgoing, 'expert', split_axis=0, concat_axis=0, tiled=True)  5.49 us
  transfers between devices with their start and end apart: 4, of which 4 were waited for; matrix products, arithmetic and copies ran while one was open for 4% of the time, Pallas kernels for 0%

commit v1 on v0

--- a/solution.py
+++ b/solution.py
@@ -107,7 +107,12 @@
         out_weight,
         preferred_element_type=jnp.float32,
     )
-    returned_cols = lax.all_to_all(columns, "expert", split_axis=0, concat_axis=1, tiled=True)
+    returned_cols = jnp.concatenate(
+        lax.all_to_all(
+            jnp.stack(jnp.split(columns, lax.axis_size("expert"), axis=0)), "expert", 0, 0
+        ),
+        axis=1,
+    )
     mixed = lax.psum(returned_cols, "tensor").astype(jnp.bfloat16)
     hidden_state = (residual.astype(jnp.float32) + mixed.astype(jnp.float32)).astype(jnp.bfloat16)
     wide = hidden_state.astype(jnp.float32)

time: 136 us -> 140 us (1.029)
  local copies, waits for them, and re-layouts: 6.19 us -> 10.3 us
    unnamed x6 -> x13, local copies, waits for them, and re-layouts: 2.47 us -> 6.65 us
where the time goes in v1:
time: 140 us; the launch traced here: 139 us
  matrix products  43.3 us (31%)
  blocking collectives  39.2 us (28%)
  waiting for transfers between devices  19.8 us (14%)
  starting transfers between devices  17.7 us (13%)
  local copies, waits for them, and re-layouts  10.3 us (7%)
  other arithmetic  8.12 us (6%)
    all_gather x1, blocking collectives, local(): lax.all_gather(gated_out, 'expert', axis=0, tiled=True)  32.3 us
    dot_general x1, matrix products, expert_terms(): lax.dot_general(rows, up_weight, dims, preferred_element_type=jnp.float32)  11.3 us
    dot_general x1, matrix products, expert_terms(): lax.dot_general(rows, gate_weight, dims, preferred_element_type=jnp.float32)  11.3 us
    dot_general x1, matrix products, expert_terms(): jnp.dot(lower_hidden, down_weight, preferred_element_type=jnp.float32)  7.7 us
    dot_general x1, matrix products, expert_terms(): jnp.dot(upper_hidden, down_weight, preferred_element_type=jnp.float32)  7.7 us
    all_to_all x1, waiting for transfers between devices, local(): lax.all_to_all(partial_value, 'expert', split_axis=0, concat_axis=0, tile...  7.44 us
    all_to_all x1, waiting for transfers between devices, local(): lax.all_to_all(outgoing, 'expert', split_axis=0, concat_axis=0, tiled=True)  6.94 us
    unnamed x13, local copies, waits for them, and re-layouts  6.65 us
  transfers between devices with their start and end apart: 4, of which 4 were waited for; matrix products, arithmetic and copies ran while one was open for 4% of the time, Pallas kernels for 0%

profile of v1, /device:TPU:0, one launch (start us, length us, event | category | flops | bytes accessed | tf_op | source)
XLA Modules:
  0.0 139.1 jit_solution(4682257001229779239)
XLA Ops:
  0.7 0.8 copy.67
  1.4 0.8 copy.65
  2.2 1.1 fusion.39
  3.3 1.0 exponential_negate_fusion
  4.3 0.7 broadcast_subtract_fusion
  4.9 1.0 fusion.32
  6.0 0.9 fusion.37
  6.9 1.1 fusion.38
  8.0 0.8 fusion.24
  8.8 32.3 %all-gather = bf16[8,2,4096]{2,1,0:T(2,128)(2,1)S(1)} all-gather(bf16[1,2,4096]{2,1,0:T(2,128)(2,1)S(1)} %fusion.24), channel_id=1, replica_groups=mesh['groups'=2,'expert'=8,'tensor'=2] {'expert'}, dimensions={0}, use_global_device_ids=true | all-gather | bytes 147456 | tf_op jit(solution)/shard_map/all_gather | solution.py:106
  41.2 2.8 %fusion.40 = f32[16,512]{1,0:T(8,128)S(1)} fusion(bf16[16,4096]{1,0:T(8,128)(2,1)S(1)} %reshape.111, bf16[4096,512]{1,0:T(8,128)(2,1)} %param.34), kind=kOutput, calls=%fused_computation.92 | convolution fusion | flops 67108864 | bytes 4358144 | tf_op jit(solution)/shard_map/dot_general | solution.py:105
  44.0 0.6 constant_dynamic-update-slice_fusion.7
  44.7 0.6 constant_dynamic-update-slice_fusion.6
  45.2 0.6 constant_dynamic-update-slice_fusion.5
  45.8 0.6 constant_dynamic-update-slice_fusion.4
  46.4 0.6 constant_dynamic-update-slice_fusion.3
  47.0 0.6 constant_dynamic-update-slice_fusion.2
  47.6 0.6 constant_dynamic-update-slice_fusion.1
  48.2 0.6 constant_dynamic-update-slice_fusion
  48.8 5.5 %all-to-all-start = ((f32[8,2,512]{2,1,0:T(2,128)}), f32[8,2,512]{2,1,0:T(2,128)S(1)}, u32[]{:S(2)}, u32[]{:S(2)}) async-start(f32[8,2,512]{2,1,0:T(2,128)} %constant_dynamic-update-slice_fusion), calls=%async_computation | async-start | bytes 65536 | tf_op jit(solution)/shard_map/all_to_all | solution.py:111
  54.3 0.7 convert_element_type.85
  55.0 0.8 convert_reduce_fusion
  55.7 0.2 convolution_compare_fusion
  55.9 0.1 copy.70
  56.0 5.0 %all-to-all-done = f32[8,2,512]{2,1,0:T(2,128)S(1)} async-done(((f32[8,2,512]{2,1,0:T(2,128)}), f32[8,2,512]{2,1,0:T(2,128)S(1)}, u32[]{:S(2)}, u32[]{:S(2)}) %all-to-all-start) | async-done | bytes 32800 | tf_op jit(solution)/shard_map/all_to_all | solution.py:111
  61.0 0.6 broadcast_in_dim.29
  61.6 3.3 %all-to-all-start.1 = ((bf16[8,2,3]{2,1,0:T(2,128)(2,1)}), bf16[8,2,3]{2,1,0:T(2,128)(2,1)S(1)}, u32[]{:S(2)}, u32[]{:S(2)}) async-start(bf16[8,2,3]{2,1,0:T(2,128)(2,1)} %broadcast_in_dim.29), calls=%async_computation.1 | async-start | bytes 8192 | tf_op jit(solution)/shard_map/all_to_all | solution.py:142
  64.9 3.4 %psum.14 = bf16[2,4096]{1,0:T(2,128)(2,1)S(1)} all-reduce(f32[2,4096]{1,0:T(2,128)S(1)} %bitcast.88), channel_id=1, replica_groups=mesh['groups'=2,'expert'=8,'tensor'=2] {'tensor'}, use_global_device_ids=true, to_apply=%region_1.2 | all-reduce | flops 8192 | bytes 49152 | tf_op jit(solution)/shard_map/psum | solution.py:116
  68.3 0.9 fusion.13
  69.2 0.8 fusion.15
  70.0 0.8 broadcast_select_fusion
  70.8 0.4 all-to-all-done.1
  71.2 5.5 %all-to-all-start.2 = ((bf16[8,2,4096]{2,1,0:T(2,128)(2,1)}), bf16[8,2,4096]{2,1,0:T(2,128)(2,1)S(1)}, u32[]{:S(2)}, u32[]{:S(2)}) async-start(bf16[8,2,4096]{2,1,0:T(2,128)(2,1)} %broadcast_select_fusion), calls=%async_computation.2 | async-start | bytes 262144 | tf_op jit(solution)/shard_map/all_to_all | solution.py:141
  76.8 0.1 copy.68
  76.9 0.1 fusion.27
  76.9 0.1 copy.71
  77.3 6.9 %all-to-all-done.2 = bf16[8,2,4096]{2,1,0:T(2,128)(2,1)S(1)} async-done(((bf16[8,2,4096]{2,1,0:T(2,128)(2,1)}), bf16[8,2,4096]{2,1,0:T(2,128)(2,1)S(1)}, u32[]{:S(2)}, u32[]{:S(2)}) %all-to-all-start.2) | async-done | bytes 131104 | tf_op jit(solution)/shard_map/all_to_all | solution.py:141
  84.3 11.3 %fusion.41 = f32[16,2304]{1,0:T(8,128)S(1)} fusion(bf16[16,4096]{1,0:T(8,128)(2,1)S(1)} %reshape.108, bf16[2304,4096]{1,0:T(8,128)(2,1)} %param.39), kind=kOutput, calls=%fused_computation.93 | convolution fusion | flops 301989888 | bytes 19152896 | tf_op jit(solution)/shard_map/dot_general | solution.py:40
  95.6 11.3 %fusion.2 = bf16[16,2304]{1,0:T(8,128)(2,1)S(1)} fusion(bf16[16,4096]{1,0:T(8,128)(2,1)S(1)} %reshape.108, bf16[2304,4096]{1,0:T(8,128)(2,1)} %param.40, f32[16,2304]{1,0:T(8,128)S(1)} %fusion.41), kind=kOutput, calls=%fused_computation.6 | convolution fusion | flops 302211072 | bytes 19226624 | tf_op jit(solution)/shard_map/dot_general | solution.py:41
  107.0 7.7 %convolution_multiply_fusion.2 = f32[16,4096]{1,0:T(8,128)S(1)} fusion(bf16[2304,4096]{1,0:T(8,128)(2,1)} %param.41, f32[16]{0:T(128)S(1)} %mul.245, bf16[16,2304]{1,0:T(8,128)(2,1)S(1)} %fusion.2, pred[2304]{0:T(1024)(128)(4,1)S(1)} %get-tuple-element.38), kind=kOutput, calls=%fused_computation.4 | convolution fusion | flops 302092288 | bytes 19212608 | tf_op jit(solution)/shard_map/dot_general | solution.py:56
  114.7 7.7 %fusion.1 = f32[16,4096]{1,0:T(8,128)S(1)} fusion(f32[16,4096]{1,0:T(8,128)S(1)} %convolution_multiply_fusion.2, bf16[2304,4096]{1,0:T(8,128)(2,1)} %param.41, f32[16]{0:T(128)S(1)} %mul.262, bf16[16,2304]{1,0:T(8,128)(2,1)S(1)} %fusion.2, pred[2304]{0:T(1024)(128)(4,1)S(1)} %get-tuple-element.37), kind=kOutput, calls=%fused_computation.3 | convolution fusion | flops 302157824 | bytes 19474752 | tf_op jit(solution)/shard_map/dot_general | solution.py:57
  122.4 0.8 reshape.109
  123.2 3.4 %all-to-all-start.3 = ((f32[8,2,4096]{2,1,0:T(2,128)}), f32[8,2,4096]{2,1,0:T(2,128)S(1)}, u32[]{:S(2)}, u32[]{:S(2)}) async-start(f32[8,2,4096]{2,1,0:T(2,128)} %reshape.109), calls=%async_computation.3 | async-start | bytes 524288 | tf_op jit(solution)/shard_map/all_to_all | solution.py:147
  126.6 0.9 copy.72
  127.5 7.4 %all-to-all-done.3 = f32[8,2,4096]{2,1,0:T(2,128)S(1)} async-done(((f32[8,2,4096]{2,1,0:T(2,128)}), f32[8,2,4096]{2,1,0:T(2,128)S(1)}, u32[]{:S(2)}, u32[]{:S(2)}) %all-to-all-start.3) | async-done | bytes 262176 | tf_op jit(solution)/shard_map/all_to_all | solution.py:147
  134.9 0.1 reduce_sum.69
  135.0 3.4 %psum.15 = f32[2,4096]{1,0:T(2,128)S(1)} all-reduce(f32[2,4096]{1,0:T(2,128)S(1)} %reduce_sum.69), channel_id=1, replica_groups=mesh['groups'=2,'expert'=8,'tensor'=2] {'tensor'}, use_global_device_ids=true, to_apply=%region_8.9 | all-reduce | flops 8192 | bytes 65536 | tf_op jit(solution)/shard_map/psum | solution.py:148
  138.4 0.6 fusion.16
  (12 shorter events, 0.4 us)
Async XLA Ops:
  0.6 6.3 %copy-start = (bf16[2,16,4096]{2,1,0:T(8,128)(2,1)S(1)}, bf16[2,16,4096]{2,1,0:T(8,128)(2,1)}, u32[]{:S(2)}) copy-start(bf16[2,16,4096]{2,1,0:T(8,128)(2,1)} %param.27) | copy-start | bytes 786436
  48.8 12.1 %all-to-all-start = ((f32[8,2,512]{2,1,0:T(2,128)}), f32[8,2,512]{2,1,0:T(2,128)S(1)}, u32[]{:S(2)}, u32[]{:S(2)}) async-start(f32[8,2,512]{2,1,0:T(2,128)} %constant_dynamic-update-slice_fusion), calls=%async_computation | async-start | bytes 65536 | tf_op jit(solution)/shard_map/all_to_all | solution.py:111
  61.6 9.7 %all-to-all-start.1 = ((bf16[8,2,3]{2,1,0:T(2,128)(2,1)}), bf16[8,2,3]{2,1,0:T(2,128)(2,1)S(1)}, u32[]{:S(2)}, u32[]{:S(2)}) async-start(bf16[8,2,3]{2,1,0:T(2,128)(2,1)} %broadcast_in_dim.29), calls=%async_computation.1 | async-start | bytes 8192 | tf_op jit(solution)/shard_map/all_to_all | solution.py:142
  71.2 13.0 %all-to-all-start.2 = ((bf16[8,2,4096]{2,1,0:T(2,128)(2,1)}), bf16[8,2,4096]{2,1,0:T(2,128)(2,1)S(1)}, u32[]{:S(2)}, u32[]{:S(2)}) async-start(bf16[8,2,4096]{2,1,0:T(2,128)(2,1)} %broadcast_select_fusion), calls=%async_computation.2 | async-start | bytes 262144 | tf_op jit(solution)/shard_map/all_to_all | solution.py:141
  123.2 11.7 %all-to-all-start.3 = ((f32[8,2,4096]{2,1,0:T(2,128)}), f32[8,2,4096]{2,1,0:T(2,128)S(1)}, u32[]{:S(2)}, u32[]{:S(2)}) async-start(f32[8,2,4096]{2,1,0:T(2,128)} %reshape.109), calls=%async_computation.3 | async-start | bytes 524288 | tf_op jit(solution)/shard_map/all_to_all | solution.py:147
